TPU v7x, 32 devices: a whole 2x2x4 slice. The times are simulated.
32 devices in a mesh: groups: 2 (over y), band: 4 (over z), head: 4 (over x, core).
Axes of the slice: x: 2, y: 2, z: 4, core: 2. Of those that a mesh axis runs over, the one named last changes fastest.
Arguments:
- latent: bfloat16 [24, 128, 1280], P(('groups', 'band'), None, 'head'), parts along dimension 0, may hold values from -80 to 80
- first_gain: float32 [1280], P('head'), may hold values from 0.1 to 1.9
- first_shift: float32 [1280], P('head'), may hold values from -3 to 3
- kernel: bfloat16 [1280, 3, 3, 1280], P('head'), may hold values from -0.0546875 to 0.0546875
- kernel_bias: float32 [1280], P('head'), may hold values from -3 to 3
- second_gain: float32 [1280], P('head'), may hold values from 0.1 to 1.9
- second_shift: float32 [1280], P('head'), may hold values from -3 to 3
- projection: bfloat16 [1280, 3, 1024], P('band', None, 'head'), may hold values from -0.8385255 to 0.8385255
- output_weight: bfloat16 [1280, 1024], P('head'), may hold values from -0.1875 to 0.1875
- output_bias: float32 [1280], P('head'), may hold values from -3 to 3
Outputs:
- convolved: bfloat16 [24, 128, 1280], P(('groups', 'band'), None, 'head'), parts along dimension 0
- attended: bfloat16 [24, 128, 1280], P(('groups', 'band'), None, 'head'), parts along dimension 0
There are 2 independent parts, one for each index of `groups`. A program takes and returns all parts, laid end to end along the dimension named above; an argument that names none is the same for every part. Nothing has to cross between parts.
All inputs are finite; a program needn't handle non-finite values.
Results may differ from a plain program's by a relative error of at most 0.012.
Values may be sent and summed in bfloat16 or wider, within the bound.
A program may use at most 128 MiB of HBM per device.

v0:
```python
import jax
import jax.numpy as jnp
from jax import lax
from jax.sharding import PartitionSpec as P

CHANNELS = 1280
HEAD_SIZE = 64
NORM_GROUPS = 32


def padded_2(cells, sides, width):
    for axis, dim in sides:
        count = lax.axis_size(axis)
        ends = count - 1
        head = lax.slice_in_dim(cells, 0, width, axis=dim)
        tail = lax.slice_in_dim(cells, cells.shape[dim] - width, cells.shape[dim], axis=dim)
        cells = jnp.concatenate(
            [
                lax.ppermute(tail, axis, [(i, (i + 1) % count) for i in range(ends)]),
                cells,
                lax.ppermute(head, axis, [((i + 1) % count, i) for i in range(ends)]),
            ],
            axis=dim,
        )
    return cells


def normalize(values, gain, shift, group_width, count):
    band_rows, width, channels = values.shape
    grouped = values.reshape(band_rows * width, channels // group_width, group_width)
    mean = lax.psum(jnp.sum(grouped, axis=(0, 2)), "band") / count
    centered = grouped - mean[None, :, None]
    spread = lax.psum(jnp.sum(centered * centered, axis=(0, 2)), "band") / count
    scaled = centered * lax.rsqrt(spread + 1e-05)[None, :, None]
    return scaled.reshape(band_rows, width, channels) * gain + shift


def contract_last(left, right):
    return lax.dot_general(
        left, right, (((1,), (1,)), ((), ())), preferred_element_type=jnp.float32
    )


def kernel_block(padded, weights, band_rows, width):
    inputs = padded.shape[2]
    wide = jnp.pad(padded, ((0, 0), (1, 1), (0, 0)))
    summed = jnp.zeros((band_rows * width, weights.shape[0]), jnp.float32)
    for above in range(3):
        for beside in range(3):
            window = wide[above : above + band_rows, beside : beside + width, :].reshape(
                band_rows * width, inputs
            )
            summed = summed + contract_last(window, weights[:, above, beside, :])
    return summed


def shards(
    latent,
    first_gain,
    first_shift,
    kernel,
    kernel_bias,
    second_gain,
    second_shift,
    projection,
    output_weight,
    output_bias,
):
    band_rows, width, channels = latent.shape
    tokens = band_rows * width
    group_width = CHANNELS // NORM_GROUPS
    count = lax.axis_size("band") * band_rows * width * group_width
    outputs = kernel.shape[0]
    latent_wide = latent.astype(jnp.float32)
    activated = jax.nn.silu(
        normalize(latent_wide, first_gain, first_shift, group_width, count)
    ).astype(jnp.bfloat16)
    gathered = lax.all_gather(activated, "head", axis=2, tiled=True)
    padded = padded_2(gathered, (("band", 0),), 1)
    summed = kernel_block(padded, kernel, band_rows, width)
    convolved = (latent_wide + kernel_bias + summed.reshape(band_rows, width, outputs)).astype(
        jnp.bfloat16
    )
    normed = normalize(
        convolved.astype(jnp.float32), second_gain, second_shift, group_width, count
    ).astype(jnp.bfloat16)
    features = lax.all_gather(normed, "head", axis=2, tiled=True).reshape(tokens, CHANNELS)
    local_inner = projection.shape[2]
    local_heads = local_inner // HEAD_SIZE
    piece = lax.all_gather(projection, "band", axis=0, tiled=True)
    projected = jnp.dot(
        features, piece.reshape(piece.shape[0], 3 * local_inner), preferred_element_type=jnp.float32
    )
    projected = projected.astype(jnp.bfloat16).reshape(tokens, 3, local_inner)
    query = projected[:, 0].reshape(tokens, local_heads, HEAD_SIZE)
    key_value = projected[:, 1:]
    factor = HEAD_SIZE ** (-0.5)
    piece = lax.all_gather(key_value, "band", axis=0, tiled=True)
    running = jnp.full((local_heads, tokens), -1e30, jnp.float32)
    keys = piece[:, 0].reshape(piece.shape[0], local_heads, HEAD_SIZE)
    values = piece[:, 1].reshape(piece.shape[0], local_heads, HEAD_SIZE)
    scores = jnp.einsum("qhd,khd->hqk", query, keys, preferred_element_type=jnp.float32) * factor
    highest = jnp.maximum(running, jnp.max(scores, axis=2))
    weights = jnp.exp(scores - highest[:, :, None])
    total = jnp.sum(weights, axis=2)
    summed_values = jnp.einsum(
        "hqk,khd->hqd", weights.astype(jnp.bfloat16), values, preferred_element_type=jnp.float32
    )
    running, total, summed_values = (highest, total, summed_values)
    attention = (
        jnp.transpose(summed_values / total[:, :, None], (1, 0, 2))
        .reshape(tokens, local_inner)
        .astype(jnp.bfloat16)
    )
    outgoing = contract_last(lax.all_gather(attention, "head", axis=1, tiled=True), output_weight)
    attended = (
        convolved.astype(jnp.float32) + output_bias + outgoing.reshape(band_rows, width, outputs)
    )
    return (convolved, attended.astype(jnp.bfloat16))


def solution(mesh):
    placed = (
        P(("groups", "band"), None, "head"),
        P("head"),
        P("head"),
        P("head", None, None, None),
        P("head"),
        P("head"),
        P("head"),
        P("band", None, "head"),
        P("head", None),
        P("head"),
    )
    return jax.shard_map(
        shards,
        mesh=mesh,
        in_specs=placed,
        out_specs=(P(("groups", "band"), None, "head"), P(("groups", "band"), None, "head")),
        check_vma=False,
    )
```

profile of v0, /device:TPU:1, one launch (start us, length us, event | category | flops | bytes accessed | tf_op | source)
XLA Modules:
  0.0 164.2 jit_solution(207283483787826930)
XLA Ops:
  7.2 1.2 copy.40
  8.4 0.1 convert_reduce_fusion.1
  8.5 0.1 reduce_sum.55
  8.6 0.1 reduce_sum.59
  8.7 10.8 %psum.28 = f32[8]{0:T(128)S(1)} all-reduce(f32[8]{0:T(128)S(1)} %reduce_sum.59), channel_id=1, replica_groups=mesh['groups'=2,'band'=4,'head'=4] {'band'}, use_global_device_ids=true, to_apply=%region_2.0 | all-reduce | flops 8 | bytes 64 | tf_op jit(solution)/shard_map/psum | solution.py:31
  19.5 0.1 sub.36
  19.6 0.1 sub.37
  19.7 0.1 fusion.68
  19.8 0.1 reduce_sum.61
  19.9 0.1 reduce_sum.62
  20.0 6.6 %psum.29 = f32[8]{0:T(128)S(1)} all-reduce(f32[8]{0:T(128)S(1)} %reduce_sum.62), channel_id=1, replica_groups=mesh['groups'=2,'band'=4,'head'=4] {'band'}, use_global_device_ids=true, to_apply=%region_5.6 | all-reduce | flops 8 | bytes 64 | tf_op jit(solution)/shard_map/psum | solution.py:33
  26.6 0.1 mul.61
  26.7 0.1 mul.62
  26.8 0.9 fusion.76
  27.7 0.2 copy.41
  27.9 14.0 %all_gather.15 = bf16[3,128,1280]{1,2,0:T(8,128)(2,1)S(1)} all-gather(bf16[3,128,320]{1,2,0:T(8,128)(2,1)S(1)} %copy.41), channel_id=1, replica_groups=mesh['groups'=2,'band'=4,'head'=4] {'head'}, dimensions={2}, use_global_device_ids=true | all-gather | bytes 1228800 | tf_op jit(solution)/shard_map/all_gather | solution.py:78
  41.9 0.6 copy.42
  42.5 3.6 %collective-permute-start = (bf16[1,128,1280]{2,1,0:T(8,128)(2,1)S(1)}, bf16[1,128,1280]{2,1,0:T(8,128)(2,1)S(1)}, u32[]{:S(2)}, u32[]{:S(2)}) collective-permute-start(bf16[1,128,1280]{2,1,0:T(8,128)(2,1)S(1)} %get-tuple-element.20), channel_id=1, source_target_pairs={{0,4},{4,8},{8,12},{1,5},{5,9},{9,13},{2,6},{6,10},{10,14},{3,7},{... | collective-permute-start | bytes 983048 | tf_op jit(solution)/shard_map/ppermute | solution.py:19
  46.2 1.3 collective-permute-start.1
  47.5 1.7 %fusion.29 = f32[384,320]{0,1:T(8,128)S(1)} fusion(bf16[384,1280]{1,0:T(8,128)(2,1)S(1)} %bitcast.76, bf16[320,3,3,1280]{3,0,2,1:T(8,128)(2,1)} %param.13), kind=kOutput, calls=%fused_computation.36 | convolution fusion | flops 314572800 | bytes 2293760 | tf_op jit(solution)/shard_map/dot_general | solution.py:39
  49.3 3.8 %collective-permute-done = bf16[1,128,1280]{2,1,0:T(8,128)(2,1)S(1)} collective-permute-done((bf16[1,128,1280]{2,1,0:T(8,128)(2,1)S(1)}, bf16[1,128,1280]{2,1,0:T(8,128)(2,1)S(1)}, u32[]{:S(2)}, u32[]{:S(2)}) %collective-permute-start) | collective-permute-done | bytes 327712 | tf_op jit(solution)/shard_map/ppermute | solution.py:19
  53.1 3.8 %collective-permute-done.1 = bf16[1,128,1280]{2,1,0:T(8,128)(2,1)S(1)} collective-permute-done((bf16[1,128,1280]{2,1,0:T(8,128)(2,1)S(1)}, bf16[1,128,1280]{2,1,0:T(8,128)(2,1)S(1)}, u32[]{:S(2)}, u32[]{:S(2)}) %collective-permute-start.1) | collective-permute-done | bytes 327712 | tf_op jit(solution)/shard_map/ppermute | solution.py:21
  56.9 0.4 fusion.9
  57.3 0.7 fusion.83
  58.0 1.2 slice-done.1
  59.2 0.6 fusion.31
  59.8 0.6 fusion.33
  60.5 0.2 pad_maximum_fusion.1
  60.6 0.6 fusion.35
  61.2 0.6 fusion.22
  61.9 0.6 fusion.26
  62.5 0.6 fusion.24
  63.1 0.7 fusion.48
  63.8 0.6 fusion.12
  64.4 0.2 copy.48
  64.7 0.1 convert_reduce_fusion
  64.8 0.1 reduce_sum.80
  64.9 0.1 reduce_sum.81
  65.0 7.3 %psum.30 = f32[8]{0:T(128)S(1)} all-reduce(f32[8]{0:T(128)S(1)} %reduce_sum.81), channel_id=1, replica_groups=mesh['groups'=2,'band'=4,'head'=4] {'band'}, use_global_device_ids=true, to_apply=%region_8.9 | all-reduce | flops 8 | bytes 64 | tf_op jit(solution)/shard_map/psum | solution.py:31
  72.4 0.1 sub.41
  72.4 0.1 fusion.64
  72.6 0.1 reduce_sum.83
  72.6 0.1 reduce_sum.84
  72.8 8.4 %psum.31 = f32[8]{0:T(128)S(1)} all-reduce(f32[8]{0:T(128)S(1)} %reduce_sum.84), channel_id=1, replica_groups=mesh['groups'=2,'band'=4,'head'=4] {'band'}, use_global_device_ids=true, to_apply=%region_11.12 | all-reduce | flops 8 | bytes 64 | tf_op jit(solution)/shard_map/psum | solution.py:33
  81.2 0.1 mul.69
  81.3 0.1 mul.70
  81.4 0.1 fusion.67
  81.5 0.2 copy.49
  81.7 14.0 %all_gather.16 = bf16[3,128,1280]{1,2,0:T(8,128)(2,1)S(1)} all-gather(bf16[3,128,320]{1,2,0:T(8,128)(2,1)S(1)} %copy.49), channel_id=1, replica_groups=mesh['groups'=2,'band'=4,'head'=4] {'head'}, dimensions={2}, use_global_device_ids=true | all-gather | bytes 1228800 | tf_op jit(solution)/shard_map/all_gather | solution.py:87
  95.7 1.3 copy.50
  97.0 2.7 %copy.51 = bf16[1280,3,256]{0,2,1:T(8,128)(2,1)S(1)} copy(bf16[1280,3,256]{2,0,1:T(8,128)(2,1)} %all-gather.3.cloned.1.call-done) | data formatting | bytes 3932160 | tf_op jit(solution)/shard_map/all_gather | solution.py:90
  99.6 3.0 %convolution_convert_fusion = bf16[384,768]{1,0:T(8,128)(2,1)} fusion(bf16[384,1280]{1,0:T(8,128)(2,1)} %bitcast.90, bf16[1280,768]{0,1:T(8,128)(2,1)S(1)} %bitcast.84), kind=kOutput, calls=%fused_computation.13 | convolution fusion | flops 755269632 | bytes 3538944 | tf_op jit(solution)/shard_map/dot_general | solution.py:91
  102.6 1.4 copy.52
  104.0 0.8 slice.107
  104.8 0.9 copy.54
  105.7 33.8 %all-gather.5.cloned.1.call-done = bf16[1536,2,256]{0,2,1:T(8,128)(2,1)} async-done(((bf16[384,2,256]{0,2,1:T(8,128)(2,1)}), bf16[1536,2,256]{0,2,1:T(8,128)(2,1)}) %all-gather.5.cloned.1.call-update) | async-done | bytes 1572880 | tf_op jit(solution)/shard_map/all_gather | solution.py:98
  139.5 1.5 fusion.84
  141.0 1.5 multiply_reduce_fusion
  142.5 1.7 %fusion = f32[4,384]{1,0:T(4,128)S(1)} fusion(f32[4,384,1536]{2,1,0:T(8,128)S(1)} %get-tuple-element.23, f32[4,384]{1,0:T(4,128)S(1)} %broadcast_maximum_fusion), kind=kLoop, calls=%fused_computation.2 | loop fusion | flops 7076352 | bytes 9449472 | tf_op jit(solution)/shard_map/reduce_sum | solution.py:105
  144.2 2.1 %fusion.19 = bf16[384,4,64]{0,2,1:T(8,128)(2,1)S(1)} fusion(bf16[1536,4,64]{0,2,1:T(8,128)(2,1)S(1)} %bitcast.92, f32[4,384,1536]{2,1,0:T(8,128)S(1)} %get-tuple-element.23, f32[4,384]{1,0:T(4,128)S(1)} %broadcast_maximum_fusion, f32[384,4]{0,1:T(4,128)S(1)} %bitcast.97), kind=kOutput, calls=%fused_computation.20 | convolution fusion | flops 309264384 | bytes 10432512 | tf_op jit(solution)/shard_map/hqk,khd->hqd/dot_general | solution.py:106
  146.3 9.6 %all_gather.19 = bf16[384,1024]{0,1:T(8,128)(2,1)S(1)} all-gather(bf16[384,256]{0,1:T(8,128)(2,1)S(1)} %bitcast.96), channel_id=1, replica_groups=mesh['groups'=2,'band'=4,'head'=4] {'head'}, dimensions={1}, use_global_device_ids=true | all-gather | bytes 983040 | tf_op jit(solution)/shard_map/all_gather | solution.py:115
  155.8 0.6 fusion.86
  156.5 0.1 fusion.80
  156.5 0.9 copy.55
  (27 shorter events, 0.3 us)
Async XLA Ops:
  7.2 148.7 %copy-start = (bf16[320,1024]{1,0:T(8,128)(2,1)S(1)}, bf16[320,1024]{1,0:T(8,128)(2,1)}, u32[]{:S(2)}) copy-start(bf16[320,1024]{1,0:T(8,128)(2,1)} %param.18) | copy-start | bytes 1966084
  7.2 89.8 %all-gather.3.cloned.1.call-start = ((), (), s32[]{:S(2)}) async-start(), calls=%async_computation | async-start | bytes 2457600 | tf_op jit(solution)/shard_map/all_gather | solution.py:90
  42.5 10.5 %collective-permute-start = (bf16[1,128,1280]{2,1,0:T(8,128)(2,1)S(1)}, bf16[1,128,1280]{2,1,0:T(8,128)(2,1)S(1)}, u32[]{:S(2)}, u32[]{:S(2)}) collective-permute-start(bf16[1,128,1280]{2,1,0:T(8,128)(2,1)S(1)} %get-tuple-element.20), channel_id=1, source_target_pairs={{0,4},{4,8},{8,12},{1,5},{5,9},{9,13},{2,6},{6,10},{10,14},{3,7},{... | collective-permute-start | bytes 983048 | tf_op jit(solution)/shard_map/ppermute | solution.py:19
  46.2 10.7 %collective-permute-start.1 = (bf16[1,128,1280]{2,1,0:T(8,128)(2,1)S(1)}, bf16[1,128,1280]{2,1,0:T(8,128)(2,1)S(1)}, u32[]{:S(2)}, u32[]{:S(2)}) collective-permute-start(bf16[1,128,1280]{2,1,0:T(8,128)(2,1)S(1)} %get-tuple-element.21), channel_id=1, source_target_pairs={{4,0},{8,4},{12,8},{5,1},{9,5},{13,9},{6,2},{10,6},{14,10},{7,3},{... | collective-permute-start | bytes 983048 | tf_op jit(solution)/shard_map/ppermute | solution.py:21
  47.5 92.0 %all-gather.5.cloned.1.call-start = ((), (), s32[]{:S(2)}) async-start(), calls=%async_computation.1 | async-start | bytes 1966080 | tf_op jit(solution)/shard_map/all_gather | solution.py:98
  49.3 8.7 %slice-start = ((s8[7372800]{0:T(1024)(128)(4,1)}), s8[4194304]{0:T(1024)(128)(4,1)S(1)}, s32[]{:S(2)}) async-start(s8[7372800]{0:T(1024)(128)(4,1)} %bitcast.94), calls=%async_computation.2 | async-start | bytes 8388608
  57.3 1.9 %slice-start.1 = ((s8[7372800]{0:T(1024)(128)(4,1)}), s8[3178496]{0:T(1024)(128)(4,1)S(1)}, s32[]{:S(2)}) async-start(s8[7372800]{0:T(1024)(128)(4,1)} %bitcast.94), calls=%async_computation.3 | async-start | bytes 6356992
  61.9 2.8 %copy-start.1 = (f32[320]{0:T(512)S(1)}, f32[320]{0:T(512)}, u32[]{:S(2)}) copy-start(f32[320]{0:T(512)} %param.14) | copy-start | bytes 3844
  62.5 18.9 %copy-start.2 = (f32[320]{0:T(512)S(1)}, f32[320]{0:T(512)}, u32[]{:S(2)}) copy-start(f32[320]{0:T(512)} %param.16) | copy-start | bytes 3844
  62.5 18.9 %copy-start.3 = (f32[320]{0:T(512)S(1)}, f32[320]{0:T(512)}, u32[]{:S(2)}) copy-start(f32[320]{0:T(512)} %param.15) | copy-start | bytes 3844
  144.2 12.3 %copy-start.4 = (f32[320]{0:T(512)S(1)}, f32[320]{0:T(512)}, u32[]{:S(2)}) copy-start(f32[320]{0:T(512)} %param.19) | copy-start | bytes 3844
Sparse Core Ops, SparseCore 0:
  47.6 43.2 all-gather.2
  104.9 34.5 all-gather.4
where the time goes:
time: 165 us; the launch traced here: 164 us
  blocking collectives  70.7 us (43%)
  waiting for transfers between devices  41.4 us (25%)
  local copies, waits for them, and re-layouts  14.6 us (9%)
  between operations  14.3 us (9%)
  matrix products  13.9 us (8%)
  starting transfers between devices  4.99 us (3%)
  other arithmetic  4.36 us (3%)
    all_gather x1, waiting for transfers between devices, shards(): piece = lax.all_gather(key_value, 'band', axis=0, tiled=True)  33.8 us
    psum x2, blocking collectives, normalize(): mean = lax.psum(jnp.sum(grouped, axis=(0, 2)), 'band') / count  18.1 us
    psum x2, blocking collectives, normalize(): spread = lax.psum(jnp.sum(centered * centered, axis=(0, 2)), 'band') / count  15 us
    all_gather x1, blocking collectives, shards(): lax.all_gather(normed, 'head', axis=2, tiled=True).reshape(tokens, CHANNELS)  14 us
    all_gather x1, blocking collectives, shards(): gathered = lax.all_gather(activated, 'head', axis=2, tiled=True)  14 us
    all_gather x1, blocking collectives, shards(): lax.all_gather(attention, 'head', axis=1, tiled=True)  9.58 us
    dot_general x10, matrix products, contract_last(): lax.dot_general(left, right, (((1,), (1,)), ((), ())), preferred_element_...  7.28 us
    unnamed x17, local copies, waits for them, and re-layouts  4.16 us
  transfers between devices with their start and end apart: 4, of which 3 were waited for; matrix products, arithmetic and copies ran while one was open for 7% of the time, Pallas kernels for 0%

commit v1 on v0

--- a/solution.py
+++ b/solution.py
@@ -1,9 +1,15 @@
+import functools
+import math
+
 import jax
 import jax.numpy as jnp
 from jax import lax
+from jax.experimental import pallas as pl
+from jax.experimental.pallas import tpu as pltpu
 from jax.sharding import PartitionSpec as P
 
 CHANNELS = 1280
+HEADS = 16
 HEAD_SIZE = 64
 NORM_GROUPS = 32
 
@@ -119,6 +125,414 @@
     return (convolved, attended.astype(jnp.bfloat16))
 
 
+def pair_kernel(
+    shape,
+    lat_ref,
+    prm_ref,
+    kw_hbm,
+    pj_hbm,
+    ow_hbm,
+    conv_ref,
+    att_ref,
+    kw,
+    pw,
+    ow,
+    stat_a,
+    stat_b,
+    grid_in,
+    norm_in,
+    qkv_out,
+    qkv_in,
+    att_out,
+    att_in,
+    local_sem,
+    send_sem,
+    recv_sem,
+):
+    parts, bands, heads, rows, local, width = shape
+    channels = local * heads
+    tokens = rows * width
+    groups_here = local // (CHANNELS // NORM_GROUPS)
+    group_width = local // groups_here
+    g, b, h = lax.axis_index("groups"), lax.axis_index("band"), lax.axis_index("head")
+    sibling = h + 1 - 2 * lax.rem(h, 2)
+    cross = lax.rem(h + 2, heads)
+    far = lax.rem(sibling + 2, heads)
+    used = [0]
+
+    def remote(src, dst, groups=None, band=None, head=None):
+        index = used[0]
+        used[0] += 1
+        return pltpu.make_async_remote_copy(
+            src_ref=src,
+            dst_ref=dst,
+            send_sem=send_sem.at[index],
+            recv_sem=recv_sem.at[index],
+            device_id=(
+                g if groups is None else groups,
+                b if band is None else band,
+                h if head is None else head,
+            ),
+            device_id_type=pl.DeviceIdType.MESH,
+        )
+
+    opened = []
+
+    def begin(copy, sends=None):
+        opened.append((copy, sends))
+        if sends is None:
+            copy.start()
+        else:
+
+            @pl.when(sends)
+            def _():
+                copy.start()
+
+    def channel_rows(shard):
+        return pl.ds(pl.multiple_of(shard * local, local), local)
+
+    band_peers = [lax.rem(b + step, bands) for step in range(1, bands)]
+    band_sources = [lax.rem(b - step + bands, bands) for step in range(1, bands)]
+    part_peers = [lax.rem(g + step, parts) for step in range(1, parts)]
+    part_sources = [lax.rem(g - step + parts, parts) for step in range(1, parts)]
+
+    load_kernel = pltpu.make_async_copy(kw_hbm, kw, local_sem.at[0])
+    load_output = pltpu.make_async_copy(ow_hbm, ow, local_sem.at[1])
+    load_rows = pltpu.make_async_copy(pj_hbm, pw.at[:, channel_rows(b), :], local_sem.at[2])
+    load_kernel.start()
+    load_output.start()
+    load_rows.start()
+
+    barrier = pltpu.get_barrier_semaphore()
+    neighbours = (
+        [(g, b, sibling), (g, b, cross)]
+        + [(g, peer, h) for peer in band_peers]
+        + [(peer, b, h) for peer in part_peers]
+    )
+    for neighbour in neighbours:
+        pl.semaphore_signal(
+            barrier, inc=1, device_id=neighbour, device_id_type=pl.DeviceIdType.MESH
+        )
+
+    def statistics(read, stat):
+        values = [
+            read(row).astype(jnp.float32).reshape(groups_here, group_width, width)
+            for row in range(rows)
+        ]
+        count = rows * width * group_width
+        total = sum(jnp.sum(value, axis=1) for value in values)
+        mean = jnp.sum(total, axis=1, keepdims=True) / count
+        mean = jnp.broadcast_to(mean, (groups_here, width))
+        squares = 0.0
+        for value in values:
+            centered = value - mean[:, None, :]
+            squares = squares + jnp.sum(centered * centered, axis=1)
+        squares = jnp.sum(squares, axis=1, keepdims=True)
+        stat[b, 0] = mean
+        stat[b, 1] = jnp.broadcast_to(squares, (groups_here, width))
+
+    def exchange(stat):
+        return [remote(stat.at[b], stat.at[b], band=peer) for peer in band_peers]
+
+    def combined(stat):
+        count = rows * width * group_width
+        means = [stat[index, 0] for index in range(bands)]
+        mean = sum(means) / bands
+        spread = 0.0
+        for index in range(bands):
+            offset = means[index] - mean
+            spread = spread + (stat[index, 1] + offset * offset * count)
+        return mean, lax.rsqrt(spread / (count * bands) + 1e-05)
+
+    def normalized(value, mean, scale, gain, shift):
+        grouped = value.astype(jnp.float32).reshape(groups_here, group_width, width)
+        scaled = (grouped - mean[:, None, :]) * scale[:, None, :]
+        return scaled.reshape(local, width) * gain + shift
+
+    params = prm_ref[...]
+    padded = jnp.concatenate(
+        [params, jnp.zeros((128 - params.shape[0], params.shape[1]), jnp.float32)], axis=0
+    )
+    columns = padded.T
+    column = lambda index: columns[:local, index : index + 1]
+
+    statistics(lambda row: lat_ref[row], stat_a)
+    pl.semaphore_wait(barrier, len(neighbours))
+    first = exchange(stat_a)
+    for copy in first:
+        begin(copy)
+    for copy in first:
+        copy.wait_recv()
+
+    mean, scale = combined(stat_a)
+    mine, crossed, sibs, fars = (channel_rows(s) for s in (h, cross, sibling, far))
+    for row in range(rows):
+        value = normalized(lat_ref[row], mean, scale, column(0), column(1))
+        grid_in[row + 1, mine, :] = (value / (1.0 + jnp.exp(-value))).astype(jnp.bfloat16)
+
+    def gather_pieces(buffer, pieces):
+        sent = []
+        for piece in pieces:
+            own = buffer.at[piece, mine, :]
+            there = buffer.at[piece, crossed, :]
+            sent.append(
+                (
+                    remote(own, own, head=cross),
+                    remote(own, own, head=sibling),
+                    remote(there, there, head=sibling),
+                )
+            )
+        return sent
+
+    edges = (pl.ds(rows, 1), pl.ds(1, 1), pl.ds(2, rows - 2))
+    gathered = gather_pieces(grid_in, edges)
+    below, above = lax.rem(b + 1, bands), lax.rem(b + bands - 1, bands)
+    halo = []
+    for source, target, peer, sends, receives in (
+        (rows, 0, below, b < bands - 1, b > 0),
+        (1, rows + 1, above, b > 0, b < bands - 1),
+    ):
+        for shard in (mine, crossed):
+            move = remote(grid_in.at[source, shard, :], grid_in.at[target, shard, :], band=peer)
+            onward = grid_in.at[target, shard, :]
+            halo.append((move, remote(onward, onward, head=sibling), sends, receives))
+    for to_cross, to_sibling, _ in gathered:
+        begin(to_cross)
+        begin(to_sibling)
+    for index in (0, 2):
+        move, _, sends, _ = halo[index]
+        begin(move, sends)
+
+    share = local // parts
+
+    def share_rows(band, part):
+        return pl.ds(pl.multiple_of(band * local + part * share, share), share)
+
+    weights = [
+        remote(
+            pj_hbm.at[:, pl.ds(pl.multiple_of(g * share, share), share), :],
+            pw.at[:, share_rows(b, g), :],
+            band=peer,
+        )
+        for peer in band_peers
+    ]
+    for index, (to_cross, _, onward) in enumerate(gathered):
+        to_cross.wait_recv()
+        begin(onward)
+        if index < 2:
+            move, _, sends, _ = halo[2 * index + 1]
+            begin(move, sends)
+
+    for copy in weights:
+        begin(copy)
+
+    for target, receives in ((0, b > 0), (rows + 1, b < bands - 1)):
+
+        @pl.when(jnp.logical_not(receives))
+        def _(target=target):
+            grid_in[target] = jnp.zeros((channels, width), jnp.bfloat16)
+
+    for move, onward, _, receives in halo:
+
+        @pl.when(receives)
+        def _(move=move):
+            move.wait_recv()
+
+        begin(onward, receives)
+
+    for _, to_sibling, onward in gathered:
+        to_sibling.wait_recv()
+        onward.wait_recv()
+    for _, onward, _, receives in halo:
+
+        @pl.when(receives)
+        def _(onward=onward):
+            onward.wait_recv()
+
+    load_kernel.wait()
+    taps = []
+    for beside in range(3):
+        summed = None
+        for over in range(3):
+            window = jnp.concatenate([grid_in[over + row] for row in range(rows)], axis=1)
+            part = jnp.dot(kw[over, beside], window, preferred_element_type=jnp.float32)
+            summed = part if summed is None else summed + part
+        taps.append(summed)
+    place = lax.broadcasted_iota(jnp.int32, (local, width), 1)
+    bias = column(2)
+    for row in range(rows):
+        span = slice(row * width, (row + 1) * width)
+        left = jnp.where(place == 0, 0.0, pltpu.roll(taps[0][:, span], 1, 1))
+        right = jnp.where(place == width - 1, 0.0, pltpu.roll(taps[2][:, span], width - 1, 1))
+        value = lat_ref[row].astype(jnp.float32) + bias + (taps[1][:, span] + left + right)
+        conv_ref[row] = value.astype(jnp.bfloat16)
+
+    statistics(lambda row: conv_ref[row], stat_b)
+    second = exchange(stat_b)
+    for copy in second:
+        begin(copy)
+
+    passed = []
+    for copy, source in zip(weights, band_sources):
+        copy.wait_recv()
+        onward = pw.at[:, share_rows(source, g), :]
+        for peer in part_peers:
+            move = remote(onward, onward, groups=peer)
+            begin(move)
+            passed.append(move)
+
+    for copy in second:
+        copy.wait_recv()
+    mean, scale = combined(stat_b)
+    for row in range(rows):
+        value = normalized(conv_ref[row], mean, scale, column(3), column(4))
+        norm_in[row, mine, :] = value.astype(jnp.bfloat16)
+    normed = gather_pieces(norm_in, (pl.ds(0, rows),))
+    for to_cross, to_sibling, onward in normed:
+        begin(to_cross)
+        begin(to_sibling)
+        to_cross.wait_recv()
+        begin(onward)
+    load_rows.wait()
+    for move in passed:
+        move.wait_recv()
+    for to_cross, to_sibling, onward in normed:
+        to_sibling.wait_recv()
+        onward.wait_recv()
+
+    features = jnp.concatenate([norm_in[row] for row in range(rows)], axis=1)
+    contract_first = lambda left, right: lax.dot_general(
+        left, right, (((0,), (0,)), ((), ())), preferred_element_type=jnp.float32
+    )
+    for kind in range(3):
+        made = contract_first(pw[kind], features).astype(jnp.bfloat16)
+        for head in range(bands):
+            qkv_out[head, kind * HEAD_SIZE : (kind + 1) * HEAD_SIZE, :] = made[
+                head * HEAD_SIZE : (head + 1) * HEAD_SIZE
+            ]
+    spread = [remote(qkv_out.at[peer], qkv_in.at[b], band=peer) for peer in band_peers]
+    for copy in spread:
+        begin(copy)
+    qkv_in[b] = qkv_out[b]
+    for copy in spread:
+        copy.wait_recv()
+
+    keys = jnp.concatenate([qkv_in[s, HEAD_SIZE : 2 * HEAD_SIZE, :] for s in range(bands)], axis=1)
+    values = jnp.concatenate([qkv_in[s, 2 * HEAD_SIZE :, :] for s in range(bands)], axis=1)
+    keys = keys.T
+    inner = bands * HEAD_SIZE
+    feature_rows = lambda shard: pl.ds(pl.multiple_of(shard * inner, inner), inner)
+    my_head = pl.ds(pl.multiple_of(h * inner + b * HEAD_SIZE, HEAD_SIZE), HEAD_SIZE)
+    factor = HEAD_SIZE ** (-0.5) * math.log2(math.e)
+    returned = [
+        remote(att_out.at[step], att_in.at[my_head, :], band=peer)
+        for step, peer in enumerate(band_peers)
+    ]
+    for step in range(1, bands + 1):
+        peer = lax.rem(b + step, bands)
+        query = qkv_in[peer, :HEAD_SIZE, :]
+        scores = jnp.dot(keys, query, preferred_element_type=jnp.float32)
+        top = jnp.max(scores, axis=0, keepdims=True)
+        heavy = jnp.exp2((scores - top) * factor)
+        total = jnp.sum(heavy, axis=0, keepdims=True)
+        mixed = jnp.dot(values, heavy.astype(jnp.bfloat16), preferred_element_type=jnp.float32)
+        result = (mixed / total).astype(jnp.bfloat16)
+        if step < bands:
+            att_out[step - 1] = result
+            begin(returned[step - 1])
+        else:
+            att_in[my_head, :] = result
+
+    for copy in returned:
+        copy.wait_recv()
+    own, there = att_in.at[feature_rows(h), :], att_in.at[feature_rows(cross), :]
+    to_cross = remote(own, own, head=cross)
+    to_sibling = remote(own, own, head=sibling)
+    onward = remote(there, there, head=sibling)
+    begin(to_cross)
+    begin(to_sibling)
+    to_cross.wait_recv()
+    begin(onward)
+    load_output.wait()
+    to_sibling.wait_recv()
+    onward.wait_recv()
+    outgoing = jnp.dot(ow[...], att_in[...], preferred_element_type=jnp.float32)
+    bias = column(5)
+    for row in range(rows):
+        span = slice(row * width, (row + 1) * width)
+        value = conv_ref[row].astype(jnp.float32) + bias + outgoing[:, span]
+        att_ref[row] = value.astype(jnp.bfloat16)
+
+    for copy, sends in opened:
+        if sends is None:
+            copy.wait_send()
+        else:
+
+            @pl.when(sends)
+            def _(copy=copy):
+                copy.wait_send()
+
+
+def pair_shards(
+    parts,
+    bands,
+    heads,
+    latent,
+    first_gain,
+    first_shift,
+    kernel,
+    kernel_bias,
+    second_gain,
+    second_shift,
+    projection,
+    output_weight,
+    output_bias,
+):
+    rows, width, local = latent.shape
+    channels, tokens = local * heads, rows * width
+    inner = projection.shape[2]
+    groups_here = local // (CHANNELS // NORM_GROUPS)
+    vectors = [first_gain, first_shift, kernel_bias, second_gain, second_shift, output_bias]
+    params = jnp.pad(jnp.stack(vectors), ((0, 2), (0, -local % 128)))
+    vmem = pl.BlockSpec(memory_space=pltpu.VMEM)
+    hbm = pl.BlockSpec(memory_space=pl.ANY)
+    result = jax.ShapeDtypeStruct((rows, local, width), jnp.bfloat16)
+    copies = 64
+    call = pl.pallas_call(
+        functools.partial(pair_kernel, (parts, bands, heads, rows, local, width)),
+        out_shape=(result, result),
+        in_specs=[vmem, vmem, hbm, hbm, hbm],
+        out_specs=(vmem, vmem),
+        scratch_shapes=[
+            pltpu.VMEM((3, 3, local, channels), jnp.bfloat16),
+            pltpu.VMEM((3, channels, inner), jnp.bfloat16),
+            pltpu.VMEM((local, inner * heads), jnp.bfloat16),
+            pltpu.VMEM((bands, 2, groups_here, width), jnp.float32),
+            pltpu.VMEM((bands, 2, groups_here, width), jnp.float32),
+            pltpu.VMEM((rows + 2, channels, width), jnp.bfloat16),
+            pltpu.VMEM((rows, channels, width), jnp.bfloat16),
+            pltpu.VMEM((bands, 3 * HEAD_SIZE, tokens), jnp.bfloat16),
+            pltpu.VMEM((bands, 3 * HEAD_SIZE, tokens), jnp.bfloat16),
+            pltpu.VMEM((bands - 1, HEAD_SIZE, tokens), jnp.bfloat16),
+            pltpu.VMEM((inner * heads, tokens), jnp.bfloat16),
+            pltpu.SemaphoreType.DMA((3,)),
+            pltpu.SemaphoreType.DMA((copies,)),
+            pltpu.SemaphoreType.DMA((copies,)),
+        ],
+        compiler_params=pltpu.CompilerParams(
+            collective_id=0, has_side_effects=True, vmem_limit_bytes=60 << 20
+        ),
+    )
+    convolved, attended = call(
+        jnp.transpose(latent, (0, 2, 1)),
+        params,
+        jnp.transpose(kernel, (1, 2, 0, 3)),
+        jnp.transpose(projection, (1, 0, 2)),
+        output_weight,
+    )
+    return jnp.transpose(convolved, (0, 2, 1)), jnp.transpose(attended, (0, 2, 1))
+
+
 def solution(mesh):
     placed = (
         P(("groups", "band"), None, "head"),
@@ -132,8 +546,11 @@
         P("head", None),
         P("head"),
     )
+    parts, bands, heads = (mesh.shape[axis] for axis in ("groups", "band", "head"))
+    paired = heads == 4 and bands > 1 and HEADS == heads * bands and CHANNELS % (16 * parts * heads) == 0
+    body = functools.partial(pair_shards, parts, bands, heads) if paired else shards
     return jax.shard_map(
-        shards,
+        body,
         mesh=mesh,
         in_specs=placed,
         out_specs=(P(("groups", "band"), None, "head"), P(("groups", "band"), None, "head")),

time: 165 us -> 90.1 us (0.55)
  Pallas kernels: 0 us -> 81.1 us
  blocking collectives: 70.7 us -> 0 us
  waiting for transfers between devices: 41.4 us -> 0 us
  matrix products: 13.9 us -> 0 us
  between operations: 14.3 us -> 0.64 us
  local copies, waits for them, and re-layouts: 14.6 us -> 8.04 us
  starting transfers between devices: 4.99 us -> 0 us
  other arithmetic: 4.36 us -> 0 us
    pallas_call x0 -> x1, Pallas kernels: none -> 81.1 us  [pair_shards(): call(jnp.transpose(latent, (0, 2, 1)), params, jnp.transpose(kernel, (1,...]
    all_gather x3 -> x0, blocking collectives: 37.6 us -> none  [the longest x1 14 us: shards(): lax.all_gather(normed, 'head', axis=2, tiled=True).reshape(tokens, CHANNELS)]
    all_gather x2 -> x0, waiting for transfers between devices: 33.8 us -> none  [the longest x1 33.8 us: shards(): piece = lax.all_gather(key_value, 'band', axis=0, tiled=True)]
    psum x4 -> x0, blocking collectives: 33.1 us -> none  [the longest x2 18.1 us: normalize(): mean = lax.psum(jnp.sum(grouped, axis=(0, 2)), 'band') / count]
    dot_general x13 -> x0, matrix products: 13.9 us -> none  [the longest x10 7.28 us: contract_last(): lax.dot_general(left, right, (((1,), (1,)), ((), ())), preferred_element_...]
    ppermute x2 -> x0, waiting for transfers between devices: 7.6 us -> none  [the longest x1 3.81 us: padded_2(): lax.ppermute(head, axis, [((i + 1) % count, i) for i in range(ends)])]
    ppermute x2 -> x0, starting transfers between devices: 4.91 us -> none  [the longest x1 3.61 us: padded_2(): lax.ppermute(tail, axis, [(i, (i + 1) % count) for i in range(ends)])]
    all_gather x3 -> x0, local copies, waits for them, and re-layouts: 4.57 us -> none  [the longest x1 2.67 us: shards(): piece = lax.all_gather(projection, 'band', axis=0, tiled=True)]
  transfers between devices with their start and end apart: 4 -> 0, of which waited for: 3 -> 0; matrix products, arithmetic and copies ran while one was open for 7% -> 0% of each run, Pallas kernels for 0% -> 0%
where the time goes in v1:
time: 90.1 us; the launch traced here: 89.8 us
  Pallas kernels  81.1 us (90%)
  local copies, waits for them, and re-layouts  8.04 us (9%)
    pallas_call x1, Pallas kernels, pair_shards(): call(jnp.transpose(latent, (0, 2, 1)), params, jnp.transpose(kernel, (1,...  81.1 us
    another operation x7, local copies, waits for them, and re-layouts, pair_shards(): params = jnp.pad(jnp.stack(vectors), ((0, 2), (0, -local % 128)))  4.13 us
    unnamed x2, local copies, waits for them, and re-layouts  3.31 us

profile of v1, /device:TPU:1, one launch (start us, length us, event | category | flops | bytes accessed | tf_op | source)
XLA Modules:
  0.0 89.8 jit_solution(8665646042833588432)
XLA Ops:
  0.6 0.7 stack.21
  1.3 0.7 stack.22
  2.0 0.7 stack.23
  2.7 0.7 stack.24
  3.4 0.7 stack.25
  4.0 0.7 stack.26
  4.8 0.6 pad.4.prm_ref
  5.4 81.1 %shard_map.113 = (bf16[3,320,128]{2,1,0:T(8,128)(2,1)}, bf16[3,320,128]{2,1,0:T(8,128)(2,1)}) custom-call(bf16[3,320,128]{2,1,0:T(8,128)(2,1)} %bitcast.7, f32[8,384]{1,0:T(8,128)} %pad.4.prm_ref, bf16[3,3,320,1280]{3,2,1,0:T(8,128)(2,1)} %bitcast.5, bf16[3,320,256]{2,1,0:T(8,128)(2,1)} %bitcast.6, bf16[320,1024]{1,0:T(8,128)(2,1)} %ow_hbm.1), custom_call_target="tpu_custom_call" | custom-call | tf_op jit(solution)/shard_map/pallas_call | solution.py:526
  86.5 1.7 %copy.14 = bf16[3,128,320]{1,2,0:T(8,128)(2,1)} copy(bf16[3,128,320]{1,2,0:T(8,128)(2,1)} %bitcast.9) | data formatting | bytes 491520
  88.1 1.7 %copy.15 = bf16[3,128,320]{1,2,0:T(8,128)(2,1)} copy(bf16[3,128,320]{1,2,0:T(8,128)(2,1)} %bitcast.8) | data formatting | bytes 491520
  (1 shorter events, 0.0 us)

commit v2 on v1

--- a/solution.py
+++ b/solution.py
@@ -132,8 +132,8 @@
     kw_hbm,
     pj_hbm,
     ow_hbm,
-    conv_ref,
-    att_ref,
+    wide_ref,
+    gain_ref,
     kw,
     pw,
     ow,
@@ -145,6 +145,7 @@
     qkv_in,
     att_out,
     att_in,
+    conv_ref,
     local_sem,
     send_sem,
     recv_sem,
@@ -250,16 +251,37 @@
         return scaled.reshape(local, width) * gain + shift
 
     params = prm_ref[...]
+    lanes = params.shape[1]
     padded = jnp.concatenate(
-        [params, jnp.zeros((128 - params.shape[0], params.shape[1]), jnp.float32)], axis=0
+        [params, jnp.zeros((lanes - params.shape[0], lanes), jnp.float32)], axis=0
     )
     columns = padded.T
-    column = lambda index: columns[:local, index : index + 1]
+    blocks = -(-local // lanes)
+
+    def column(index):
+        pieces = [columns[:, index * blocks + k : index * blocks + k + 1] for k in range(blocks)]
+        return jnp.concatenate(pieces, axis=0)[:local]
 
     statistics(lambda row: lat_ref[row], stat_a)
     pl.semaphore_wait(barrier, len(neighbours))
     first = exchange(stat_a)
     for copy in first:
+        begin(copy)
+
+    share = local // parts
+
+    def share_rows(band, part):
+        return pl.ds(pl.multiple_of(band * local + part * share, share), share)
+
+    weights = [
+        remote(
+            pj_hbm.at[:, pl.ds(pl.multiple_of(g * share, share), share), :],
+            pw.at[:, share_rows(b, g), :],
+            band=peer,
+        )
+        for peer in band_peers
+    ]
+    for copy in weights:
         begin(copy)
     for copy in first:
         copy.wait_recv()
@@ -303,19 +325,6 @@
         move, _, sends, _ = halo[index]
         begin(move, sends)
 
-    share = local // parts
-
-    def share_rows(band, part):
-        return pl.ds(pl.multiple_of(band * local + part * share, share), share)
-
-    weights = [
-        remote(
-            pj_hbm.at[:, pl.ds(pl.multiple_of(g * share, share), share), :],
-            pw.at[:, share_rows(b, g), :],
-            band=peer,
-        )
-        for peer in band_peers
-    ]
     for index, (to_cross, _, onward) in enumerate(gathered):
         to_cross.wait_recv()
         begin(onward)
@@ -323,9 +332,6 @@
             move, _, sends, _ = halo[2 * index + 1]
             begin(move, sends)
 
-    for copy in weights:
-        begin(copy)
-
     for target, receives in ((0, b > 0), (rows + 1, b < bands - 1)):
 
         @pl.when(jnp.logical_not(receives))
@@ -348,6 +354,15 @@
         @pl.when(receives)
         def _(onward=onward):
             onward.wait_recv()
+
+    passed = []
+    for copy, source in zip(weights, band_sources):
+        copy.wait_recv()
+        onward = pw.at[:, share_rows(source, g), :]
+        for peer in part_peers:
+            move = remote(onward, onward, groups=peer)
+            begin(move)
+            passed.append(move)
 
     load_kernel.wait()
     taps = []
@@ -365,21 +380,13 @@
         left = jnp.where(place == 0, 0.0, pltpu.roll(taps[0][:, span], 1, 1))
         right = jnp.where(place == width - 1, 0.0, pltpu.roll(taps[2][:, span], width - 1, 1))
         value = lat_ref[row].astype(jnp.float32) + bias + (taps[1][:, span] + left + right)
+        wide_ref[row] = value
         conv_ref[row] = value.astype(jnp.bfloat16)
 
     statistics(lambda row: conv_ref[row], stat_b)
     second = exchange(stat_b)
     for copy in second:
         begin(copy)
-
-    passed = []
-    for copy, source in zip(weights, band_sources):
-        copy.wait_recv()
-        onward = pw.at[:, share_rows(source, g), :]
-        for peer in part_peers:
-            move = remote(onward, onward, groups=peer)
-            begin(move)
-            passed.append(move)
 
     for copy in second:
         copy.wait_recv()
@@ -404,64 +411,113 @@
     contract_first = lambda left, right: lax.dot_general(
         left, right, (((0,), (0,)), ((), ())), preferred_element_type=jnp.float32
     )
+    spread = []
     for kind in range(3):
         made = contract_first(pw[kind], features).astype(jnp.bfloat16)
         for head in range(bands):
-            qkv_out[head, kind * HEAD_SIZE : (kind + 1) * HEAD_SIZE, :] = made[
-                head * HEAD_SIZE : (head + 1) * HEAD_SIZE
-            ]
-    spread = [remote(qkv_out.at[peer], qkv_in.at[b], band=peer) for peer in band_peers]
-    for copy in spread:
-        begin(copy)
-    qkv_in[b] = qkv_out[b]
-    for copy in spread:
-        copy.wait_recv()
-
-    keys = jnp.concatenate([qkv_in[s, HEAD_SIZE : 2 * HEAD_SIZE, :] for s in range(bands)], axis=1)
-    values = jnp.concatenate([qkv_in[s, 2 * HEAD_SIZE :, :] for s in range(bands)], axis=1)
-    keys = keys.T
+            qkv_out[head, kind] = made[head * HEAD_SIZE : (head + 1) * HEAD_SIZE]
+        qkv_in[b, kind] = qkv_out[b, kind]
+        moves = [
+            remote(qkv_out.at[peer, kind], qkv_in.at[b, kind], band=peer) for peer in band_peers
+        ]
+        for copy in moves:
+            begin(copy)
+        spread.append(moves)
+
     inner = bands * HEAD_SIZE
-    feature_rows = lambda shard: pl.ds(pl.multiple_of(shard * inner, inner), inner)
-    my_head = pl.ds(pl.multiple_of(h * inner + b * HEAD_SIZE, HEAD_SIZE), HEAD_SIZE)
     factor = HEAD_SIZE ** (-0.5) * math.log2(math.e)
+
+    def feature_rows(shard, band):
+        return pl.ds(pl.multiple_of(shard * inner + band * HEAD_SIZE, HEAD_SIZE), HEAD_SIZE)
+
+    sources = [b] + band_sources
+    onwards = [lax.rem(b + step, bands) for step in range(bands)]
+    queries, keys, values, running = [], [], [], []
+
+    def attend(index, chunks):
+        scores = [
+            jnp.dot(keys[c], queries[index], preferred_element_type=jnp.float32) for c in chunks
+        ]
+        top = functools.reduce(
+            jnp.maximum, [jnp.max(score, axis=0, keepdims=True) for score in scores]
+        )
+        before = running[index]
+        if before is not None:
+            top = jnp.maximum(top, before[0])
+        total, mixed = 0.0, 0.0
+        for c, score in zip(chunks, scores):
+            heavy = jnp.exp2((score - top) * factor)
+            total = total + jnp.sum(heavy, axis=0, keepdims=True)
+            mixed = mixed + jnp.dot(
+                values[c], heavy.astype(jnp.bfloat16), preferred_element_type=jnp.float32
+            )
+        if before is not None:
+            fade = jnp.exp2((before[0] - top) * factor)
+            total = total + before[1] * fade
+            mixed = mixed + before[2] * fade
+        running[index] = (top, total, mixed)
+
+    def finished(index):
+        _, total, mixed = running[index]
+        return (mixed / total).astype(jnp.bfloat16)
+
     returned = [
-        remote(att_out.at[step], att_in.at[my_head, :], band=peer)
-        for step, peer in enumerate(band_peers)
+        remote(att_out.at[index], att_in.at[feature_rows(h, b), :], band=source)
+        for index, source in enumerate(band_sources)
     ]
-    for step in range(1, bands + 1):
-        peer = lax.rem(b + step, bands)
-        query = qkv_in[peer, :HEAD_SIZE, :]
-        scores = jnp.dot(keys, query, preferred_element_type=jnp.float32)
-        top = jnp.max(scores, axis=0, keepdims=True)
-        heavy = jnp.exp2((scores - top) * factor)
-        total = jnp.sum(heavy, axis=0, keepdims=True)
-        mixed = jnp.dot(values, heavy.astype(jnp.bfloat16), preferred_element_type=jnp.float32)
-        result = (mixed / total).astype(jnp.bfloat16)
-        if step < bands:
-            att_out[step - 1] = result
-            begin(returned[step - 1])
-        else:
-            att_in[my_head, :] = result
-
-    for copy in returned:
-        copy.wait_recv()
-    own, there = att_in.at[feature_rows(h), :], att_in.at[feature_rows(cross), :]
-    to_cross = remote(own, own, head=cross)
-    to_sibling = remote(own, own, head=sibling)
-    onward = remote(there, there, head=sibling)
-    begin(to_cross)
-    begin(to_sibling)
-    to_cross.wait_recv()
-    begin(onward)
+    final = []
+    for source in onwards:
+        own = att_in.at[feature_rows(h, source), :]
+        there = att_in.at[feature_rows(cross, source), :]
+        final.append(
+            (
+                remote(own, own, head=cross),
+                remote(own, own, head=sibling),
+                remote(there, there, head=sibling),
+            )
+        )
+
+    def pass_on(index):
+        if index > 0:
+            returned[index - 1].wait_recv()
+        begin(final[index][0])
+        begin(final[index][1])
+
+    def relay(index):
+        final[index][0].wait_recv()
+        begin(final[index][2])
+
+    for index in range(bands):
+        if index > 0:
+            for moves in spread:
+                moves[index - 1].wait_recv()
+        source = sources[index]
+        queries.append(qkv_in[source, 0])
+        keys.append(qkv_in[source, 1].T)
+        values.append(qkv_in[source, 2])
+        running.append(None)
+        last = index == bands - 1
+        for earlier in list(range(1, index)) + [index] + ([0] if index > 0 else []):
+            attend(earlier, list(range(index + 1)) if earlier == index else [index])
+            if last:
+                if earlier > 0:
+                    att_out[earlier - 1] = finished(earlier)
+                    begin(returned[earlier - 1])
+                else:
+                    att_in[feature_rows(h, b), :] = finished(0)
+    for index in range(bands):
+        pass_on(index)
+    for index in range(bands):
+        relay(index)
     load_output.wait()
-    to_sibling.wait_recv()
-    onward.wait_recv()
+    for _, to_sibling, onward in final:
+        to_sibling.wait_recv()
+        onward.wait_recv()
     outgoing = jnp.dot(ow[...], att_in[...], preferred_element_type=jnp.float32)
     bias = column(5)
     for row in range(rows):
         span = slice(row * width, (row + 1) * width)
-        value = conv_ref[row].astype(jnp.float32) + bias + outgoing[:, span]
-        att_ref[row] = value.astype(jnp.bfloat16)
+        gain_ref[row] = outgoing[:, span] + bias
 
     for copy, sends in opened:
         if sends is None:
@@ -493,10 +549,12 @@
     inner = projection.shape[2]
     groups_here = local // (CHANNELS // NORM_GROUPS)
     vectors = [first_gain, first_shift, kernel_bias, second_gain, second_shift, output_bias]
-    params = jnp.pad(jnp.stack(vectors), ((0, 2), (0, -local % 128)))
+    gap = jnp.zeros((-local % 128,), jnp.float32)
+    flat = jnp.concatenate([piece for vector in vectors for piece in (vector, gap)])
+    params = jnp.pad(flat, (0, -flat.shape[0] % 1024)).reshape(-1, 128)
     vmem = pl.BlockSpec(memory_space=pltpu.VMEM)
     hbm = pl.BlockSpec(memory_space=pl.ANY)
-    result = jax.ShapeDtypeStruct((rows, local, width), jnp.bfloat16)
+    result = jax.ShapeDtypeStruct((rows, local, width), jnp.float32)
     copies = 64
     call = pl.pallas_call(
         functools.partial(pair_kernel, (parts, bands, heads, rows, local, width)),
@@ -511,10 +569,11 @@
             pltpu.VMEM((bands, 2, groups_here, width), jnp.float32),
             pltpu.VMEM((rows + 2, channels, width), jnp.bfloat16),
             pltpu.VMEM((rows, channels, width), jnp.bfloat16),
-            pltpu.VMEM((bands, 3 * HEAD_SIZE, tokens), jnp.bfloat16),
-            pltpu.VMEM((bands, 3 * HEAD_SIZE, tokens), jnp.bfloat16),
+            pltpu.VMEM((bands, 3, HEAD_SIZE, tokens), jnp.bfloat16),
+            pltpu.VMEM((bands, 3, HEAD_SIZE, tokens), jnp.bfloat16),
             pltpu.VMEM((bands - 1, HEAD_SIZE, tokens), jnp.bfloat16),
             pltpu.VMEM((inner * heads, tokens), jnp.bfloat16),
+            pltpu.VMEM((rows, local, width), jnp.bfloat16),
             pltpu.SemaphoreType.DMA((3,)),
             pltpu.SemaphoreType.DMA((copies,)),
             pltpu.SemaphoreType.DMA((copies,)),
@@ -523,14 +582,16 @@
             collective_id=0, has_side_effects=True, vmem_limit_bytes=60 << 20
         ),
     )
-    convolved, attended = call(
+    wide, gained = call(
         jnp.transpose(latent, (0, 2, 1)),
         params,
         jnp.transpose(kernel, (1, 2, 0, 3)),
         jnp.transpose(projection, (1, 0, 2)),
         output_weight,
     )
-    return jnp.transpose(convolved, (0, 2, 1)), jnp.transpose(attended, (0, 2, 1))
+    convolved = jnp.transpose(wide, (0, 2, 1)).astype(jnp.bfloat16)
+    attended = convolved.astype(jnp.float32) + jnp.transpose(gained, (0, 2, 1))
+    return convolved, attended.astype(jnp.bfloat16)
 
 
 def solution(mesh):

time: 90.1 us -> 86.3 us (0.958)
  local copies, waits for them, and re-layouts: 8.04 us -> 1.45 us
  other arithmetic: 0 us -> 2.02 us
    another operation x7 -> x0, local copies, waits for them, and re-layouts: 4.13 us -> none  [pair_shards(): params = jnp.pad(jnp.stack(vectors), ((0, 2), (0, -local % 128)))]
    unnamed x2 -> x0, local copies, waits for them, and re-layouts: 3.31 us -> none
    convert_element_type x0 -> x1, other arithmetic: none -> 2.02 us  [pair_shards(): return (convolved, attended.astype(jnp.bfloat16))]
where the time goes in v2:
time: 86.3 us; the launch traced here: 86.1 us
  Pallas kernels  82 us (95%)
  other arithmetic  2.02 us (2%)
  local copies, waits for them, and re-layouts  1.45 us (2%)
    pallas_call x1, Pallas kernels, pair_shards(): call(jnp.transpose(latent, (0, 2, 1)), params, jnp.transpose(kernel, (1,...  82 us
    convert_element_type x1, other arithmetic, pair_shards(): return (convolved, attended.astype(jnp.bfloat16))  2.02 us

profile of v2, /device:TPU:1, one launch (start us, length us, event | category | flops | bytes accessed | tf_op | source)
XLA Modules:
  0.0 86.1 jit_solution(7802623111812918310)
XLA Ops:
  0.6 0.8 concatenate.3
  1.5 0.6 pad_bitcast_fusion.prm_ref
  2.1 82.0 %shard_map.113 = (f32[3,320,128]{2,1,0:T(8,128)}, f32[3,320,128]{2,1,0:T(8,128)}) custom-call(bf16[3,320,128]{2,1,0:T(8,128)(2,1)} %bitcast.14, f32[24,128]{1,0:T(8,128)} %pad_bitcast_fusion.prm_ref, bf16[3,3,320,1280]{3,2,1,0:T(8,128)(2,1)} %bitcast.12, bf16[3,320,256]{2,1,0:T(8,128)(2,1)} %bitcast.13, bf16[320,1024]{1,0:T(8,128)(2,1)} %ow_hbm.1), custom_call_target="tpu_custom_call" | custom-call | tf_op jit(solution)/shard_map/pallas_call | solution.py:585
  84.1 2.0 %fusion = (bf16[3,128,320]{1,2,0:T(8,128)(2,1)}, bf16[3,128,320]{1,2,0:T(8,128)(2,1)}) fusion(f32[3,320,128]{2,1,0:T(8,128)} %get-tuple-element.5, f32[3,320,128]{2,1,0:T(8,128)} %get-tuple-element.4), kind=kLoop, calls=%fused_computation.1 | loop fusion | flops 491520 | bytes 1474560 | tf_op jit(solution)/shard_map/convert_element_type | solution.py:594
  (1 shorter events, 0.0 us)

commit v3 on v2

--- a/solution.py
+++ b/solution.py
@@ -281,8 +281,18 @@
         )
         for peer in band_peers
     ]
-    for copy in weights:
-        begin(copy)
+    order = sorted(range(bands - 1), key=lambda index: index % 2)
+    passed = []
+
+    def pass_rows(index):
+        weights[index].wait_recv()
+        onward = pw.at[:, share_rows(band_sources[index], g), :]
+        for peer in part_peers:
+            move = remote(onward, onward, groups=peer)
+            begin(move)
+            passed.append(move)
+
+    begin(weights[order[0]])
     for copy in first:
         copy.wait_recv()
 
@@ -325,6 +335,9 @@
         move, _, sends, _ = halo[index]
         begin(move, sends)
 
+    pass_rows(order[0])
+    for index in order[1:2]:
+        begin(weights[index])
     for index, (to_cross, _, onward) in enumerate(gathered):
         to_cross.wait_recv()
         begin(onward)
@@ -332,6 +345,8 @@
             move, _, sends, _ = halo[2 * index + 1]
             begin(move, sends)
 
+    for index in order[2:]:
+        begin(weights[index])
     for target, receives in ((0, b > 0), (rows + 1, b < bands - 1)):
 
         @pl.when(jnp.logical_not(receives))
@@ -355,15 +370,8 @@
         def _(onward=onward):
             onward.wait_recv()
 
-    passed = []
-    for copy, source in zip(weights, band_sources):
-        copy.wait_recv()
-        onward = pw.at[:, share_rows(source, g), :]
-        for peer in part_peers:
-            move = remote(onward, onward, groups=peer)
-            begin(move)
-            passed.append(move)
-
+    for index in order[1:2]:
+        pass_rows(index)
     load_kernel.wait()
     taps = []
     for beside in range(3):
@@ -398,6 +406,9 @@
     for to_cross, to_sibling, onward in normed:
         begin(to_cross)
         begin(to_sibling)
+    for index in order[2:]:
+        pass_rows(index)
+    for to_cross, _, onward in normed:
         to_cross.wait_recv()
         begin(onward)
     load_rows.wait()
@@ -430,37 +441,7 @@
     def feature_rows(shard, band):
         return pl.ds(pl.multiple_of(shard * inner + band * HEAD_SIZE, HEAD_SIZE), HEAD_SIZE)
 
-    sources = [b] + band_sources
     onwards = [lax.rem(b + step, bands) for step in range(bands)]
-    queries, keys, values, running = [], [], [], []
-
-    def attend(index, chunks):
-        scores = [
-            jnp.dot(keys[c], queries[index], preferred_element_type=jnp.float32) for c in chunks
-        ]
-        top = functools.reduce(
-            jnp.maximum, [jnp.max(score, axis=0, keepdims=True) for score in scores]
-        )
-        before = running[index]
-        if before is not None:
-            top = jnp.maximum(top, before[0])
-        total, mixed = 0.0, 0.0
-        for c, score in zip(chunks, scores):
-            heavy = jnp.exp2((score - top) * factor)
-            total = total + jnp.sum(heavy, axis=0, keepdims=True)
-            mixed = mixed + jnp.dot(
-                values[c], heavy.astype(jnp.bfloat16), preferred_element_type=jnp.float32
-            )
-        if before is not None:
-            fade = jnp.exp2((before[0] - top) * factor)
-            total = total + before[1] * fade
-            mixed = mixed + before[2] * fade
-        running[index] = (top, total, mixed)
-
-    def finished(index):
-        _, total, mixed = running[index]
-        return (mixed / total).astype(jnp.bfloat16)
-
     returned = [
         remote(att_out.at[index], att_in.at[feature_rows(h, b), :], band=source)
         for index, source in enumerate(band_sources)
@@ -487,27 +468,31 @@
         final[index][0].wait_recv()
         begin(final[index][2])
 
-    for index in range(bands):
+    for moves in spread:
+        for copy in moves:
+            copy.wait_recv()
+    keys = jnp.concatenate([qkv_in[source, 1] for source in range(bands)], axis=1).T
+    values = jnp.concatenate([qkv_in[source, 2] for source in range(bands)], axis=1)
+    for index in list(range(1, bands)) + [0]:
+        query = qkv_in[b if index == 0 else band_sources[index - 1], 0]
+        scores = jnp.dot(keys, query, preferred_element_type=jnp.float32)
+        top = jnp.max(scores, axis=0, keepdims=True)
+        heavy = jnp.exp2((scores - top) * factor)
+        total = jnp.sum(heavy, axis=0, keepdims=True)
+        mixed = jnp.dot(values, heavy.astype(jnp.bfloat16), preferred_element_type=jnp.float32)
+        result = (mixed / total).astype(jnp.bfloat16)
         if index > 0:
-            for moves in spread:
-                moves[index - 1].wait_recv()
-        source = sources[index]
-        queries.append(qkv_in[source, 0])
-        keys.append(qkv_in[source, 1].T)
-        values.append(qkv_in[source, 2])
-        running.append(None)
-        last = index == bands - 1
-        for earlier in list(range(1, index)) + [index] + ([0] if index > 0 else []):
-            attend(earlier, list(range(index + 1)) if earlier == index else [index])
-            if last:
-                if earlier > 0:
-                    att_out[earlier - 1] = finished(earlier)
-                    begin(returned[earlier - 1])
-                else:
-                    att_in[feature_rows(h, b), :] = finished(0)
-    for index in range(bands):
-        pass_on(index)
-    for index in range(bands):
+            att_out[index - 1] = result
+            begin(returned[index - 1])
+            if index > 1:
+                pass_on(index - 1)
+            if index > 2:
+                relay(index - 2)
+        else:
+            att_in[feature_rows(h, b), :] = result
+            pass_on(0)
+    pass_on(bands - 1)
+    for index in list(range(max(bands - 2, 1), bands)) + [0]:
         relay(index)
     load_output.wait()
     for _, to_sibling, onward in final:

time: 86.3 us -> 81.2 us (0.941)
  Pallas kernels: 82 us -> 76.9 us
    pallas_call x1, Pallas kernels: 82 us -> 76.9 us  [pair_shards(): call(jnp.transpose(latent, (0, 2, 1)), params, jnp.transpose(kernel, (1,...]
where the time goes in v3:
time: 81.2 us; the launch traced here: 81.1 us
  Pallas kernels  76.9 us (95%)
  other arithmetic  2.02 us (2%)
  local copies, waits for them, and re-layouts  1.45 us (2%)
    pallas_call x1, Pallas kernels, pair_shards(): call(jnp.transpose(latent, (0, 2, 1)), params, jnp.transpose(kernel, (1,...  76.9 us
    convert_element_type x1, other arithmetic, pair_shards(): return (convolved, attended.astype(jnp.bfloat16))  2.02 us

profile of v3, /device:TPU:1, one launch (start us, length us, event | category | flops | bytes accessed | tf_op | source)
XLA Modules:
  0.0 81.1 jit_solution(5249117603206906457)
XLA Ops:
  0.6 0.8 %concatenate.3 = f32[2304]{0:T(1024)S(1)} concatenate(f32[320]{0:T(512)} %param.11, f32[64]{0:T(128)S(1)} %broadcast_in_dim.3, f32[320]{0:T(512)} %param.12, f32[64]{0:T(128)S(1)} %broadcast_in_dim.3, f32[320]{0:T(512)} %param.14, f32[64]{0:T(128)S(1)} %broadcast_in_dim.3, f32[320]{0:T(512)} %param.15, f32[64]{0:T(128)S(1)} %broadcast_in_dim.3, f32[320]{0:T(512)} %param.16, ...), dimensions={0} | concatenate | bytes 18432 | tf_op jit(solution)/shard_map/concatenate | solution.py:538
  1.5 0.6 pad_bitcast_fusion.prm_ref
  2.1 76.9 %shard_map.113 = (f32[3,320,128]{2,1,0:T(8,128)}, f32[3,320,128]{2,1,0:T(8,128)}) custom-call(bf16[3,320,128]{2,1,0:T(8,128)(2,1)} %bitcast.14, f32[24,128]{1,0:T(8,128)} %pad_bitcast_fusion.prm_ref, bf16[3,3,320,1280]{3,2,1,0:T(8,128)(2,1)} %bitcast.12, bf16[3,320,256]{2,1,0:T(8,128)(2,1)} %bitcast.13, bf16[320,1024]{1,0:T(8,128)(2,1)} %ow_hbm.1), custom_call_target="tpu_custom_call" | custom-call | tf_op jit(solution)/shard_map/pallas_call | solution.py:570
  79.0 2.0 %fusion = (bf16[3,128,320]{1,2,0:T(8,128)(2,1)}, bf16[3,128,320]{1,2,0:T(8,128)(2,1)}) fusion(f32[3,320,128]{2,1,0:T(8,128)} %get-tuple-element.5, f32[3,320,128]{2,1,0:T(8,128)} %get-tuple-element.4), kind=kLoop, calls=%fused_computation.1 | loop fusion | flops 491520 | bytes 1474560 | tf_op jit(solution)/shard_map/convert_element_type | solution.py:579
  (1 shorter events, 0.0 us)

commit v4 on v3

--- a/solution.py
+++ b/solution.py
@@ -335,9 +335,6 @@
         move, _, sends, _ = halo[index]
         begin(move, sends)
 
-    pass_rows(order[0])
-    for index in order[1:2]:
-        begin(weights[index])
     for index, (to_cross, _, onward) in enumerate(gathered):
         to_cross.wait_recv()
         begin(onward)
@@ -345,7 +342,8 @@
             move, _, sends, _ = halo[2 * index + 1]
             begin(move, sends)
 
-    for index in order[2:]:
+    pass_rows(order[0])
+    for index in order[1:]:
         begin(weights[index])
     for target, receives in ((0, b > 0), (rows + 1, b < bands - 1)):
 
@@ -370,8 +368,6 @@
         def _(onward=onward):
             onward.wait_recv()
 
-    for index in order[1:2]:
-        pass_rows(index)
     load_kernel.wait()
     taps = []
     for beside in range(3):
@@ -395,6 +391,8 @@
     second = exchange(stat_b)
     for copy in second:
         begin(copy)
+    for index in order[1:2]:
+        pass_rows(index)
 
     for copy in second:
         copy.wait_recv()
@@ -468,17 +466,21 @@
         final[index][0].wait_recv()
         begin(final[index][2])
 
-    for moves in spread:
+    for moves in spread[:2]:
         for copy in moves:
             copy.wait_recv()
     keys = jnp.concatenate([qkv_in[source, 1] for source in range(bands)], axis=1).T
-    values = jnp.concatenate([qkv_in[source, 2] for source in range(bands)], axis=1)
+    values = None
     for index in list(range(1, bands)) + [0]:
         query = qkv_in[b if index == 0 else band_sources[index - 1], 0]
         scores = jnp.dot(keys, query, preferred_element_type=jnp.float32)
         top = jnp.max(scores, axis=0, keepdims=True)
         heavy = jnp.exp2((scores - top) * factor)
         total = jnp.sum(heavy, axis=0, keepdims=True)
+        if values is None:
+            for copy in spread[2]:
+                copy.wait_recv()
+            values = jnp.concatenate([qkv_in[source, 2] for source in range(bands)], axis=1)
         mixed = jnp.dot(values, heavy.astype(jnp.bfloat16), preferred_element_type=jnp.float32)
         result = (mixed / total).astype(jnp.bfloat16)
         if index > 0:
@@ -502,7 +504,7 @@
     bias = column(5)
     for row in range(rows):
         span = slice(row * width, (row + 1) * width)
-        gain_ref[row] = outgoing[:, span] + bias
+        gain_ref[row] = conv_ref[row].astype(jnp.float32) + bias + outgoing[:, span]
 
     for copy, sends in opened:
         if sends is None:
@@ -575,8 +577,7 @@
         output_weight,
     )
     convolved = jnp.transpose(wide, (0, 2, 1)).astype(jnp.bfloat16)
-    attended = convolved.astype(jnp.float32) + jnp.transpose(gained, (0, 2, 1))
-    return convolved, attended.astype(jnp.bfloat16)
+    return convolved, jnp.transpose(gained, (0, 2, 1)).astype(jnp.bfloat16)
 
 
 def solution(mesh):

time: 81.2 us -> 81.3 us (level)
  no operation moved by 1% of the time
where the time goes in v4:
time: 81.3 us; the launch traced here: 81.1 us
  Pallas kernels  77 us (95%)
  other arithmetic  2.02 us (2%)
  local copies, waits for them, and re-layouts  1.45 us (2%)
    pallas_call x1, Pallas kernels, pair_shards(): call(jnp.transpose(latent, (0, 2, 1)), params, jnp.transpose(kernel, (1,...  77 us
    convert_element_type x1, other arithmetic, pair_shards(): return (convolved, jnp.transpose(gained, (0, 2, 1)).astype(jnp.bfloat16))  2.02 us

profile of v4, /device:TPU:1, one launch (start us, length us, event | category | flops | bytes accessed | tf_op | source)
XLA Modules:
  0.0 81.1 jit_solution(12130986493868339320)
XLA Ops:
  0.6 0.8 %concatenate.3 = f32[2304]{0:T(1024)S(1)} concatenate(f32[320]{0:T(512)} %param.11, f32[64]{0:T(128)S(1)} %broadcast_in_dim.3, f32[320]{0:T(512)} %param.12, f32[64]{0:T(128)S(1)} %broadcast_in_dim.3, f32[320]{0:T(512)} %param.14, f32[64]{0:T(128)S(1)} %broadcast_in_dim.3, f32[320]{0:T(512)} %param.15, f32[64]{0:T(128)S(1)} %broadcast_in_dim.3, f32[320]{0:T(512)} %param.16, ...), dimensions={0} | concatenate | bytes 18432 | tf_op jit(solution)/shard_map/concatenate | solution.py:540
  1.5 0.6 pad_bitcast_fusion.prm_ref
  2.1 77.0 %shard_map.113 = (f32[3,320,128]{2,1,0:T(8,128)}, f32[3,320,128]{2,1,0:T(8,128)}) custom-call(bf16[3,320,128]{2,1,0:T(8,128)(2,1)} %bitcast.11, f32[24,128]{1,0:T(8,128)} %pad_bitcast_fusion.prm_ref, bf16[3,3,320,1280]{3,2,1,0:T(8,128)(2,1)} %bitcast.9, bf16[3,320,256]{2,1,0:T(8,128)(2,1)} %bitcast.10, bf16[320,1024]{1,0:T(8,128)(2,1)} %ow_hbm.1), custom_call_target="tpu_custom_call" | custom-call | tf_op jit(solution)/shard_map/pallas_call | solution.py:572
  79.1 2.0 %convert_bitcast_fusion = (bf16[3,128,320]{1,2,0:T(8,128)(2,1)}, bf16[3,128,320]{1,2,0:T(8,128)(2,1)}) fusion(f32[3,320,128]{2,1,0:T(8,128)} %get-tuple-element.5, f32[3,320,128]{2,1,0:T(8,128)} %get-tuple-element.4), kind=kLoop, calls=%fused_computation | loop fusion | flops 245760 | bytes 1474560 | tf_op jit(solution)/shard_map/convert_element_type | solution.py:580
  (1 shorter events, 0.0 us)

commit v5 on v4

--- a/solution.py
+++ b/solution.py
@@ -273,26 +273,48 @@
     def share_rows(band, part):
         return pl.ds(pl.multiple_of(band * local + part * share, share), share)
 
-    weights = [
-        remote(
-            pj_hbm.at[:, pl.ds(pl.multiple_of(g * share, share), share), :],
-            pw.at[:, share_rows(b, g), :],
-            band=peer,
-        )
-        for peer in band_peers
-    ]
-    order = sorted(range(bands - 1), key=lambda index: index % 2)
     passed = []
-
-    def pass_rows(index):
-        weights[index].wait_recv()
-        onward = pw.at[:, share_rows(band_sources[index], g), :]
-        for peer in part_peers:
-            move = remote(onward, onward, groups=peer)
-            begin(move)
-            passed.append(move)
-
-    begin(weights[order[0]])
+    hops = []
+    for hop in range(1, bands):
+        pair = []
+        for sign, peer in ((1, lax.rem(b + 1, bands)), (-1, lax.rem(b + bands - 1, bands))):
+            held = lax.rem(b - sign * (hop - 1) + bands, bands)
+            got = lax.rem(b - sign * hop + bands, bands)
+            if sign > 0:
+                sends = jnp.logical_and(b < bands - 1, b >= hop - 1)
+                receives = b >= hop
+            else:
+                sends = jnp.logical_and(b > 0, b + hop - 1 < bands)
+                receives = b + hop < bands
+            if hop == 1:
+                source = pj_hbm.at[:, pl.ds(pl.multiple_of(g * share, share), share), :]
+            else:
+                source = pw.at[:, share_rows(held, g), :]
+            move = remote(source, pw.at[:, share_rows(held, g), :], band=peer)
+            pair.append((move, sends, receives, got))
+        hops.append(pair)
+
+    def send_hop(index):
+        for move, sends, _, _ in hops[index]:
+            begin(move, sends)
+
+    def take_hop(index):
+        for move, _, receives, got in hops[index]:
+
+            @pl.when(receives)
+            def _(move=move):
+                move.wait_recv()
+
+        if index + 1 < len(hops):
+            send_hop(index + 1)
+        for _, _, receives, got in hops[index]:
+            onward = pw.at[:, share_rows(got, g), :]
+            for peer in part_peers:
+                move = remote(onward, onward, groups=peer)
+                begin(move, receives)
+                passed.append((move, receives))
+
+    send_hop(0)
     for copy in first:
         copy.wait_recv()
 
@@ -342,9 +364,7 @@
             move, _, sends, _ = halo[2 * index + 1]
             begin(move, sends)
 
-    pass_rows(order[0])
-    for index in order[1:]:
-        begin(weights[index])
+    take_hop(0)
     for target, receives in ((0, b > 0), (rows + 1, b < bands - 1)):
 
         @pl.when(jnp.logical_not(receives))
@@ -368,6 +388,8 @@
         def _(onward=onward):
             onward.wait_recv()
 
+    for index in range(1, min(2, len(hops))):
+        take_hop(index)
     load_kernel.wait()
     taps = []
     for beside in range(3):
@@ -391,8 +413,6 @@
     second = exchange(stat_b)
     for copy in second:
         begin(copy)
-    for index in order[1:2]:
-        pass_rows(index)
 
     for copy in second:
         copy.wait_recv()
@@ -404,14 +424,18 @@
     for to_cross, to_sibling, onward in normed:
         begin(to_cross)
         begin(to_sibling)
-    for index in order[2:]:
-        pass_rows(index)
+    for index in range(2, len(hops)):
+        take_hop(index)
     for to_cross, _, onward in normed:
         to_cross.wait_recv()
         begin(onward)
     load_rows.wait()
-    for move in passed:
-        move.wait_recv()
+    for move, receives in passed:
+
+        @pl.when(receives)
+        def _(move=move):
+            move.wait_recv()
+
     for to_cross, to_sibling, onward in normed:
         to_sibling.wait_recv()
         onward.wait_recv()
@@ -542,7 +566,7 @@
     vmem = pl.BlockSpec(memory_space=pltpu.VMEM)
     hbm = pl.BlockSpec(memory_space=pl.ANY)
     result = jax.ShapeDtypeStruct((rows, local, width), jnp.float32)
-    copies = 64
+    copies = 96
     call = pl.pallas_call(
         functools.partial(pair_kernel, (parts, bands, heads, rows, local, width)),
         out_shape=(result, result),

time: 81.3 us -> 71.3 us (0.88)
  Pallas kernels: 77 us -> 67 us
    pallas_call x1, Pallas kernels: 77 us -> 67 us  [pair_shards(): call(jnp.transpose(latent, (0, 2, 1)), params, jnp.transpose(kernel, (1,...]
where the time goes in v5:
time: 71.3 us; the launch traced here: 71.1 us
  Pallas kernels  67 us (94%)
  other arithmetic  2.02 us (3%)
  local copies, waits for them, and re-layouts  1.45 us (2%)
    pallas_call x1, Pallas kernels, pair_shards(): call(jnp.transpose(latent, (0, 2, 1)), params, jnp.transpose(kernel, (1,...  67 us
    convert_element_type x1, other arithmetic, pair_shards(): return (convolved, jnp.transpose(gained, (0, 2, 1)).astype(jnp.bfloat16))  2.02 us

profile of v5, /device:TPU:1, one launch (start us, length us, event | category | flops | bytes accessed | tf_op | source)
XLA Modules:
  0.0 71.1 jit_solution(2545006351685803336)
XLA Ops:
  0.6 0.8 %concatenate.3 = f32[2304]{0:T(1024)S(1)} concatenate(f32[320]{0:T(512)} %param.11, f32[64]{0:T(128)S(1)} %broadcast_in_dim.3, f32[320]{0:T(512)} %param.12, f32[64]{0:T(128)S(1)} %broadcast_in_dim.3, f32[320]{0:T(512)} %param.14, f32[64]{0:T(128)S(1)} %broadcast_in_dim.3, f32[320]{0:T(512)} %param.15, f32[64]{0:T(128)S(1)} %broadcast_in_dim.3, f32[320]{0:T(512)} %param.16, ...), dimensions={0} | concatenate | bytes 18432 | tf_op jit(solution)/shard_map/concatenate | solution.py:564
  1.5 0.6 pad_bitcast_fusion.prm_ref
  2.1 67.0 %shard_map.113 = (f32[3,320,128]{2,1,0:T(8,128)}, f32[3,320,128]{2,1,0:T(8,128)}) custom-call(bf16[3,320,128]{2,1,0:T(8,128)(2,1)} %bitcast.11, f32[24,128]{1,0:T(8,128)} %pad_bitcast_fusion.prm_ref, bf16[3,3,320,1280]{3,2,1,0:T(8,128)(2,1)} %bitcast.9, bf16[3,320,256]{2,1,0:T(8,128)(2,1)} %bitcast.10, bf16[320,1024]{1,0:T(8,128)(2,1)} %ow_hbm.1), custom_call_target="tpu_custom_call" | custom-call | tf_op jit(solution)/shard_map/pallas_call | solution.py:596
  69.1 2.0 %convert_bitcast_fusion = (bf16[3,128,320]{1,2,0:T(8,128)(2,1)}, bf16[3,128,320]{1,2,0:T(8,128)(2,1)}) fusion(f32[3,320,128]{2,1,0:T(8,128)} %get-tuple-element.5, f32[3,320,128]{2,1,0:T(8,128)} %get-tuple-element.4), kind=kLoop, calls=%fused_computation | loop fusion | flops 245760 | bytes 1474560 | tf_op jit(solution)/shard_map/convert_element_type | solution.py:604
  (1 shorter events, 0.0 us)
